TPU v7x, 32 devices: a whole 2x2x4 slice. The times are simulated.
32 devices in a mesh: shots: 2 (over y), depth: 2 (over core), lat: 8 (over z, x).
Axes of the slice: x: 2, y: 2, z: 4, core: 2. Of those that a mesh axis runs over, the one named last changes fastest.
Arguments:
- surface: float32 [4, 2, 1024, 1024], P('shots', None, 'lat'), parts along dimension 0, may hold values from -6 to 6
- slowness: float32 [2, 1024, 1024], P('depth', 'lat'), may hold values from 1.6 to 3.2
- stencil_coef: float32 [3, 2, 1024, 1024], P(None, 'depth', 'lat'), may hold values from 0.02 to 0.06
- base_slowness: float32 [8], replicated, may hold values from 2 to 2.8
- base_index: int32 [2], P('depth'), may hold values from 0 to 7
- frequency_table: float32 [16], replicated, may hold values from 0.6 to 1.2
- slot_frequency: int32 [4], P('shots'), parts along dimension 0, may hold values from 0 to 15
Outputs:
- migrated: float32 [4, 1024, 1024], P(('shots', 'depth'), 'lat'), parts along dimension 0
There are 2 independent parts, one for each index of `shots`. A program takes and returns all parts, laid end to end along the dimension named above; an argument that names none is the same for every part. Nothing has to cross between parts.
All inputs are finite; a program needn't handle non-finite values.
Results may differ from a plain program's by a relative error of at most 0.0003.
Values sent between devices are 32-bit elements; how exact they have to be, the bound alone decides.
A program may use at most 64 MiB of HBM per device.

v0:
```python
import math

import jax
import jax.numpy as jnp
from jax import lax
from jax.experimental import pallas as pl
from jax.experimental.pallas import tpu as pltpu
from jax.sharding import PartitionSpec as P

depth_spacing = 1.0
highest = lax.Precision.HIGHEST


def with_halo(cells, sides, width):
    for axis, dim in sides:
        count = lax.axis_size(axis)
        ends = count - 1
        head = lax.slice_in_dim(cells, 0, width, axis=dim)
        tail = lax.slice_in_dim(cells, cells.shape[dim] - width, cells.shape[dim], axis=dim)
        cells = jnp.concatenate(
            [
                lax.ppermute(tail, axis, [(i, (i + 1) % count) for i in range(ends)]),
                cells,
                lax.ppermute(head, axis, [((i + 1) % count, i) for i in range(ends)]),
            ],
            axis=dim,
        )
    return cells


def dft_table(count):
    row_index = lax.broadcasted_iota(jnp.int32, (count, count), 0)
    col_index = lax.broadcasted_iota(jnp.int32, (count, count), 1)
    angle = 2.0 * math.pi / count * (row_index * col_index % count).astype(jnp.float32)
    return (jnp.cos(angle), jnp.sin(angle))


def wavenumbers(index, count):
    signed = jnp.where(index < count // 2, index, index - count)
    return 2.0 * math.pi / count * signed.astype(jnp.float32)


def along_last(values, table):
    return jnp.einsum("brn,nk->brk", values, table, precision=highest)


def along_middle(values, table):
    return jnp.einsum("bxk,xj->bkj", values, table, precision=highest)


def pair_last(pair, table):
    batch = pair.shape[0]
    merged = pair.reshape((batch * 2,) + pair.shape[2:])
    result = along_last(merged, table)
    return result.reshape((batch, 2) + result.shape[1:])


def pair_middle(pair, table):
    batch = pair.shape[0]
    merged = pair.reshape((batch * 2,) + pair.shape[2:])
    result = along_middle(merged, table)
    return result.reshape((batch, 2) + result.shape[1:])


def stencil_sum(extended):
    center = extended[:, :, 1:-1]
    sideways = jnp.pad(center, ((0, 0), (0, 0), (0, 0), (1, 1)))
    return (
        extended[:, :, 2:]
        + extended[:, :, :-2]
        + sideways[..., 2:]
        + sideways[..., :-2]
        - 4.0 * center
    )


def correct(wavefield, stencil_value, coefficient):
    real_part = wavefield[:, 0] - coefficient[None] * stencil_value[:, 1]
    imag_part = wavefield[:, 1] + coefficient[None] * stencil_value[:, 0]
    return jnp.stack((real_part, imag_part), axis=1)


def shards(
    surface, slowness, stencil_coef, base_slowness, base_index, frequency_table, slot_frequency
):
    section_index = lax.axis_index("depth")
    sections = lax.axis_size("depth")
    lanes = lax.axis_size("lat")
    slots = surface.shape[0]
    rows = surface.shape[2]
    width_y = surface.shape[3]
    width_x = rows * lanes
    block_y = width_y // lanes
    steps_here = slowness.shape[0]
    stencils = stencil_coef.shape[0]
    cos_x, sin_x = dft_table(width_x)
    cos_y, sin_y = dft_table(width_y)
    wave_x = wavenumbers(lax.broadcasted_iota(jnp.int32, (width_x,), 0), width_x)[None, None, :]
    local_y = lax.axis_index("lat") * block_y + lax.broadcasted_iota(jnp.int32, (block_y,), 0)
    wave_y = wavenumbers(local_y, width_y)[None, :, None]
    lateral = wave_x**2 + wave_y**2
    table_freq = lax.broadcasted_iota(jnp.int32, (1, frequency_table.shape[0]), 1)
    omegas = jnp.sum(
        jnp.where(slot_frequency[:, None] == table_freq, frequency_table[None, :], 0.0), axis=1
    )
    table_base = lax.broadcasted_iota(jnp.int32, (1, base_slowness.shape[0]), 1)
    base_values = jnp.sum(
        jnp.where(base_index[:, None] == table_base, base_slowness[None, :], 0.0), axis=1
    )
    volume_slow, volume_coef, volume_base = (
        lax.all_gather(slowness, "depth", axis=0, tiled=True),
        lax.all_gather(stencil_coef, "depth", axis=1, tiled=True),
        lax.all_gather(base_values, "depth", axis=0, tiled=True),
    )
    levels = steps_here * sections
    mine = slots // sections
    first_mine = section_index * mine
    wavefield = lax.dynamic_slice_in_dim(surface, first_mine, mine, 0)
    freqs = lax.dynamic_slice_in_dim(omegas, first_mine, mine, 0)
    partial_layers = []
    for level in range(levels):
        depth_wavefield = wavefield
        batch = depth_wavefield.shape[0]
        base_value = volume_base[level]
        with_cos = pair_last(depth_wavefield, cos_y)
        with_sin = pair_last(depth_wavefield, sin_y)
        fwd_real = with_cos[:, 0] + with_sin[:, 1]
        fwd_imag = with_cos[:, 1] - with_sin[:, 0]
        packed = jnp.stack((fwd_real, fwd_imag), axis=1).reshape(batch, 2, rows, lanes, block_y)
        columns = lax.all_to_all(packed, "lat", split_axis=3, concat_axis=2, tiled=True).reshape(
            batch, 2, width_x, block_y
        )
        col_cos = pair_middle(columns, cos_x)
        col_sin = pair_middle(columns, sin_x)
        spec_real = col_cos[:, 0] + col_sin[:, 1]
        spec_imag = col_cos[:, 1] - col_sin[:, 0]
        vertical = ((freqs * base_value) ** 2)[:, None, None] - lateral
        root = jnp.sqrt(jnp.abs(vertical))
        shift_real = jnp.where(
            vertical > 0, jnp.cos(depth_spacing * root), jnp.exp(-depth_spacing * root)
        )
        shift_imag = jnp.where(vertical > 0, jnp.sin(depth_spacing * root), 0.0)
        moved = jnp.stack(
            (
                spec_real * shift_real - spec_imag * shift_imag,
                spec_real * shift_imag + spec_imag * shift_real,
            ),
            axis=1,
        )
        back_cos = pair_last(moved, cos_x)
        back_sin = pair_last(moved, sin_x)
        back_real = back_cos[:, 0] - back_sin[:, 1]
        back_imag = back_cos[:, 1] + back_sin[:, 0]
        packed = jnp.stack((back_real, back_imag), axis=1).reshape(batch, 2, block_y, lanes, rows)
        returned = lax.all_to_all(packed, "lat", split_axis=3, concat_axis=2, tiled=True).reshape(
            batch, 2, width_y, rows
        )
        scale = 1.0 / (width_x * width_y)
        ret_cos = pair_middle(returned, cos_y)
        ret_sin = pair_middle(returned, sin_y)
        out_real = (ret_cos[:, 0] - ret_sin[:, 1]) * scale
        out_imag = (ret_cos[:, 1] + ret_sin[:, 0]) * scale
        screen = depth_spacing * freqs[:, None, None] * (volume_slow[level] - base_value)[None]
        cosine = jnp.cos(screen)
        sine = jnp.sin(screen)
        depth_wavefield = jnp.stack(
            (out_real * cosine - out_imag * sine, out_real * sine + out_imag * cosine), axis=1
        )
        for stencil in range(stencils):
            extended = with_halo(depth_wavefield, (("lat", 2),), 1)
            depth_wavefield = correct(
                depth_wavefield, stencil_sum(extended), volume_coef[stencil, level]
            )
        wavefield = depth_wavefield
        partial_layers.append(jnp.sum(wavefield[:, 0], axis=0))
    partial_image = jnp.stack(partial_layers)
    return lax.psum_scatter(partial_image, "depth", scatter_dimension=0, tiled=True)


MESH = pl.DeviceIdType.MESH
tile_rows = 8
tile_lanes = 128
chunk = 16
gate_step = 3


def times_root(value, power, count, sign):
    real, imag = value
    turn = (power * 8 // count) % 8 if (power * 8) % count == 0 else None
    half = math.sqrt(0.5)
    if turn == 0:
        return value
    if turn == 2:
        return (-imag, real) if sign > 0 else (imag, -real)
    if turn == 1:
        if sign > 0:
            return ((real - imag) * half, (real + imag) * half)
        return ((real + imag) * half, (imag - real) * half)
    if turn == 3:
        if sign > 0:
            return (-(real + imag) * half, (real - imag) * half)
        return ((imag - real) * half, -(real + imag) * half)
    angle = sign * 2.0 * math.pi * power / count
    cosine, sine = math.cos(angle), math.sin(angle)
    return (real * cosine - imag * sine, real * sine + imag * cosine)


def short_dft(values, sign):
    count = len(values)
    if count == 1:
        return values
    even = short_dft(values[0::2], sign)
    odd = short_dft(values[1::2], sign)
    low, high = [], []
    for power in range(count // 2):
        turned = times_root(odd[power], power, count, sign)
        low.append((even[power][0] + turned[0], even[power][1] + turned[1]))
        high.append((even[power][0] - turned[0], even[power][1] - turned[1]))
    return low + high


def quarter_sincos(rest, quarter):
    square = rest * rest
    sine = rest + rest * square * (
        -1.6666654611e-1 + square * (8.3321608736e-3 + square * -1.9515295891e-4)
    )
    cosine = (
        1.0
        - 0.5 * square
        + square
        * square
        * (4.166664568298827e-2 + square * (-1.388731625493765e-3 + square * 2.443315711809948e-5))
    )
    swap = quarter % 2 == 1
    first = jnp.where(swap, cosine, sine)
    second = jnp.where(swap, sine, cosine)
    turn = quarter % 4
    return (
        jnp.where(turn >= 2, -first, first),
        jnp.where((turn == 1) | (turn == 2), -second, second),
    )


def sincos(angle):
    nearest = jnp.floor(angle * (2.0 / math.pi) + 0.5)
    rest = angle - nearest * 1.5703125
    rest = rest - nearest * 4.83751296997e-4
    rest = rest - nearest * 7.54978995489e-8
    return quarter_sincos(rest, nearest.astype(jnp.int32) & 3)


def split(values):
    high = values.astype(jnp.bfloat16)
    return high, (values - high.astype(jnp.float32)).astype(jnp.bfloat16)


def mul(left, right):
    return jnp.dot(left, right, preferred_element_type=jnp.float32)


def migrate_kernel(
    surface,
    slowness,
    coef,
    base_table,
    base_index,
    freq_table,
    slot_freq,
    out,
    field,
    fwd_hi,
    fwd_lo,
    bwd_hi,
    bwd_lo,
    short,
    after,
    phase,
    sent,
    got,
    back,
    ret,
    wide,
    coefs,
    slow,
    parcel,
    parcel_in,
    base,
    image,
    image_in,
    load_sem,
    vol_send,
    vol_recv,
    base_sem,
    send_sem,
    recv_sem,
    image_sem,
):
    lanes, rows2, width = short.shape
    rows = rows2 // 2
    ext = coefs.shape[2]
    halo = (ext - rows) // 2
    count = lanes * rows
    levels = coefs.shape[0]
    wire = rows + tile_rows
    half = lanes // 2
    far = lax.rem(lax.div(lax.axis_index("lat"), half) + 1, 2) * half
    near = lax.div(lax.axis_index("lat"), half) * half
    stencils = coef.shape[0]
    top = tile_rows
    own = top + halo
    me = lax.axis_index("lat")
    core = lax.axis_index("depth")
    other = 1 - core
    up = lax.rem(me + lanes - 1, lanes)
    down = lax.rem(me + 1, lanes)

    barrier = pltpu.get_barrier_semaphore()
    for step in range(1, lanes):
        pl.semaphore_signal(
            barrier,
            inc=1,
            device_id={"lat": lax.rem(me + step, lanes)},
            device_id_type=MESH,
        )
    for place in (me, up, down):
        pl.semaphore_signal(
            barrier, inc=1, device_id={"depth": other, "lat": place}, device_id_type=MESH
        )

    load = pltpu.make_async_copy(
        surface.at[core], field.at[0, :, pl.ds(own, rows), :], load_sem.at[0]
    )
    load.start()
    mine = [
        pltpu.make_async_copy(
            slowness.at[0], slow.at[core, pl.ds(0, rows), :], load_sem.at[1]
        ),
        pltpu.make_async_copy(
            coef.at[:, 0], coefs.at[core, :, pl.ds(halo, rows), :], load_sem.at[2]
        ),
    ]
    for copy in mine:
        copy.start()

    omega = freq_table[slot_freq[core]]
    base[core] = jnp.full(base.shape[1:], base_table[base_index[0]], jnp.float32)
    wide_y = field.shape[3]
    back[:, :, :, rows:, :] = jnp.zeros((levels, lanes, 2, tile_rows, width), jnp.float32)
    ret[:, :, :, rows:, :] = jnp.zeros((levels, lanes, 2, chunk, width), jnp.float32)
    slow[:, rows:, :] = jnp.zeros((levels, chunk, wide_y), jnp.float32)
    parcel[...] = jnp.zeros(parcel.shape, jnp.float32)
    rim = jnp.zeros((levels, stencils, halo, wide_y), jnp.float32)
    coefs[:, :, 0:halo, :] = rim
    coefs[:, :, halo + rows :, :] = rim
    edge = jnp.zeros((2, 2, top + halo, wide_y), jnp.float32)
    field[:, :, 0:own, :] = edge
    field[:, :, own + rows :, :] = edge

    def table(index, hi, lo, flip):
        def strip(at, carry):
            start = pl.multiple_of(at * chunk, chunk)
            row = start + lax.broadcasted_iota(jnp.int32, (chunk, width), 0)
            col = lax.broadcasted_iota(jnp.int32, (chunk, width), 1)
            power = col * (row * lanes + index) if flip else row * (col * lanes + index)
            power = power & (count - 1)
            quarter = (4 * power + count // 2) // count
            rest = power - quarter * (count // 4)
            sine, cosine = quarter_sincos(
                rest.astype(jnp.float32) * (2.0 * math.pi / count), quarter & 3
            )
            c_hi, c_lo = split(cosine)
            s_hi, s_lo = split(sine)
            n_hi, n_lo = -s_hi, -s_lo
            if flip:
                quads = ((c_hi, s_hi, n_hi, c_hi), (c_lo, s_lo, n_lo, c_lo))
            else:
                quads = ((c_hi, n_hi, s_hi, c_hi), (c_lo, n_lo, s_lo, c_lo))
            for ref, (aa, ab, ba, bb) in zip((hi, lo), quads):
                ref[index, pl.ds(start, chunk), 0:width] = aa
                ref[index, pl.ds(start, chunk), width:] = ab
                ref[index, pl.ds(rows + start, chunk), 0:width] = ba
                ref[index, pl.ds(rows + start, chunk), width:] = bb
            return carry

        lax.fori_loop(0, rows // chunk, strip, 0)

    def tables(hi, lo, flip):
        def body(index, carry):
            table(index, hi, lo, flip)
            return carry

        lax.fori_loop(0, lanes, body, 0)

    load.wait()

    def remote(src, dst, send, recv, device):
        return pltpu.make_async_remote_copy(
            src_ref=src,
            dst_ref=dst,
            send_sem=send,
            recv_sem=recv,
            device_id=device,
            device_id_type=MESH,
        )

    def volume_copies():
        whole = {"depth": other}
        found = [
            remote(base.at[core], base.at[core], base_sem.at[0], base_sem.at[1], whole),
            remote(
                slowness.at[0],
                slow.at[core, pl.ds(0, rows), :],
                vol_send.at[0],
                vol_recv.at[0],
                whole,
            ),
            remote(
                coef.at[:, 0],
                coefs.at[core, :, pl.ds(halo, rows), :],
                vol_send.at[1],
                vol_recv.at[1],
                whole,
            ),
        ]
        targets = ((core, up, 0), (other, up, 0), (core, down, 1), (other, down, 1))
        for at, (section, place, side) in enumerate(targets):
            found.append(
                remote(
                    parcel.at[side],
                    parcel_in.at[core, side],
                    vol_send.at[2 + at],
                    vol_recv.at[2 + at],
                    {"depth": section, "lat": place},
                )
            )
        return found

    def parcel_rows():
        at = 0
        for stencil in range(stencils - 1):
            size = stencils - 1 - stencil
            yield stencil, at, size
            at += size
        yield stencils, at, stencils

    def pack_parcels():
        for which, at, size in parcel_rows():
            if which < stencils:
                first = coefs[core, which, halo : halo + size, :]
                last = coefs[core, which, halo + rows - size : halo + rows, :]
            else:
                first = slow[core, 0:size, :]
                last = slow[core, rows - size : rows, :]
            parcel[0, at : at + size, :] = first
            parcel[1, at : at + size, :] = last

    def unpack_parcels():
        for level in range(levels):
            for which, at, size in parcel_rows():
                below = parcel_in[level, 0, at : at + size, :]
                above = parcel_in[level, 1, at : at + size, :]
                if which < stencils:
                    coefs[level, which, halo - size : halo, :] = above * inside_first
                    coefs[level, which, halo + rows : halo + rows + size, :] = (
                        below * inside_last
                    )
                else:
                    slow[level, rows : rows + size, :] = above
                    slow[level, rows + size : rows + 2 * size, :] = below

    inside_first = jnp.where(me > 0, 1.0, 0.0)
    inside_last = jnp.where(me < lanes - 1, 1.0, 0.0)

    def wavenumber(index):
        signed = jnp.where(index < count // 2, index, index - count)
        return 2.0 * math.pi / count * signed.astype(jnp.float32)

    def make_phase(level):
        edge_q = (omega * base[level][0:1, :]) ** 2

        def body(index, carry):
            def strip(at, inner):
                start = pl.multiple_of(at * chunk, chunk)
                row = start + lax.broadcasted_iota(jnp.int32, (chunk, width), 0)
                col = lax.broadcasted_iota(jnp.int32, (chunk, width), 1)
                lateral = (
                    wavenumber(row * lanes + index) ** 2 + wavenumber(col * lanes + me) ** 2
                )
                vertical = edge_q - lateral
                root = jnp.sqrt(jnp.abs(vertical))
                sine, cosine = sincos(depth_spacing * root)
                fade = jnp.exp(-depth_spacing * root)
                scale = 1.0 / (count * count)
                moving = vertical > 0
                phase[index, pl.ds(start, chunk), :] = jnp.where(moving, cosine, fade) * scale
                phase[index, pl.ds(rows + start, chunk), :] = (
                    jnp.where(moving, sine, 0.0) * scale
                )
                return inner

            lax.fori_loop(0, rows // chunk, strip, 0)
            return carry

        lax.fori_loop(0, lanes, body, 0)

    quarter = lax.div(me * 4, lanes)
    outer = 1 - lax.div(lax.rem(quarter + 1, 4), 2)

    def peer_at(step):
        place = lax.rem(step + outer * half, lanes - 1)
        beside = lax.div(place, half)
        return far + beside * (near - far) + lax.rem(me + place + beside, half)

    def each_peer(body, low=0, high=lanes - 1):
        def at(step, carry):
            body(peer_at(step))
            return carry

        lax.fori_loop(low, high, at, 0)

    gated = min(gate_step, lanes - 2)
    volume = volume_copies()
    swap = remote(
        image.at[other], image_in, image_sem.at[0], image_sem.at[1], {"depth": other}
    )
    for level in range(levels):
        source = 0 if level == 0 else stencils % 2

        def split_rows(at, carry):
            start = pl.multiple_of(at * chunk, chunk)
            values = [
                tuple(
                    field[source, part, pl.ds(own + start, chunk), a * width : (a + 1) * width]
                    for part in range(2)
                )
                for a in range(lanes)
            ]
            for d, (real, imag) in enumerate(short_dft(values, -1)):
                wide[d, pl.ds(start, chunk), 0:width] = real
                wide[d, pl.ds(start, chunk), width:] = imag
            return carry

        lax.fori_loop(0, rows // chunk, split_rows, 0)

        def forward(d):
            hi, lo = split(wide[d, 0:rows, :])
            made = mul(jnp.concatenate([hi, lo], axis=0), fwd_hi[d])
            return made[:rows] + made[rows:] + mul(hi, fwd_lo[d])

        if level == 0:
            pl.semaphore_wait(barrier, lanes + 2)

        def there(peer):
            return remote(
                sent.at[level, peer],
                got.at[level, me],
                send_sem.at[level, 0, peer],
                recv_sem.at[level, 0, me],
                {"lat": peer},
            )

        def send_forward(peer):
            if level == 0:
                table(peer, fwd_hi, fwd_lo, False)
            made = forward(peer)
            sent[level, peer, 0:rows, :] = made[:, 0:width]
            sent[level, peer, rows:, :] = made[:, width:]
            there(peer).start()

        def prepare():
            tables(bwd_hi, bwd_lo, True)
            volume[0].wait()
            make_phase(level)

        if level == 0:
            for copy in volume[:3]:
                copy.start()

            @pl.when(core == 1)
            def _():
                prepare()

        each_peer(send_forward)
        if level == 0:
            table(me, fwd_hi, fwd_lo, False)
        made = forward(me)
        got[level, me, 0:rows, :] = made[:, 0:width]
        got[level, me, rows:, :] = made[:, width:]

        if level == 0:
            for copy in mine:
                copy.wait()
            pack_parcels()
            for copy in volume[3:]:
                copy.start()

            @pl.when(core == 0)
            def _():
                prepare()

            there(peer_at(gated)).wait_send()
        else:
            make_phase(level)

        def arrive_forward(peer):
            remote(
                sent.at[level, me],
                got.at[level, peer],
                send_sem.at[level, 0, me],
                recv_sem.at[level, 0, peer],
                {"lat": peer},
            ).wait_recv()

        each_peer(arrive_forward)

        def split_columns(at, carry):
            start = pl.multiple_of(at * chunk, chunk)
            values = [
                (
                    got[level, r, pl.ds(start, chunk), :],
                    got[level, r, pl.ds(rows + start, chunk), :],
                )
                for r in range(lanes)
            ]
            for e, (real, imag) in enumerate(short_dft(values, -1)):
                short[e, pl.ds(start, chunk), :] = real
                short[e, pl.ds(rows + start, chunk), :] = imag
            return carry

        lax.fori_loop(0, rows // chunk, split_columns, 0)

        def left(hi_table, lo_table, values):
            hi, lo = split(values)
            made = mul(hi_table, jnp.concatenate([hi, lo], axis=1))
            return made[:, 0:width] + made[:, width:] + mul(lo_table, hi)

        def column(e, carry):
            spec = left(bwd_hi[e], bwd_lo[e], short[e])
            real, imag = spec[:rows], spec[rows:]
            shift_real, shift_imag = phase[e, 0:rows, :], phase[e, rows:, :]
            moved = jnp.concatenate(
                [
                    real * shift_real - imag * shift_imag,
                    real * shift_imag + imag * shift_real,
                ],
                axis=0,
            )
            after[e] = left(fwd_hi[e], fwd_lo[e], moved)
            return carry

        lax.fori_loop(0, lanes, column, 0)

        def join_columns(at, carry):
            start = pl.multiple_of(at * chunk, chunk)
            values = [
                (after[e, pl.ds(start, chunk), :], after[e, pl.ds(rows + start, chunk), :])
                for e in range(lanes)
            ]
            for r, (real, imag) in enumerate(short_dft(values, 1)):
                back[level, r, 0, pl.ds(start, chunk), :] = real
                back[level, r, 1, pl.ds(start, chunk), :] = imag
            return carry

        lax.fori_loop(0, rows // chunk, join_columns, 0)
        for r in range(lanes):
            for part in range(2):
                back[level, r, part, rows : rows + stencils, :] = back[
                    level, (r - 1) % lanes, part, rows - stencils : rows, :
                ]
                back[level, r, part, rows + stencils : rows + 2 * stencils, :] = back[
                    level, (r + 1) % lanes, part, 0:stencils, :
                ]

        def home(peer):
            return remote(
                back.at[level, peer],
                ret.at[level, me, :, pl.ds(0, wire), :],
                send_sem.at[level, 1, peer],
                recv_sem.at[level, 1, me],
                {"lat": peer},
            )

        each_peer(lambda peer: home(peer).start())

        def inverse(d, real, imag):
            hi, lo = split(jnp.concatenate([real, imag], axis=1))
            wide[d] = mul(hi, bwd_hi[d]) + mul(lo, bwd_hi[d]) + mul(hi, bwd_lo[d])

        for part in range(2):
            ret[level, me, part, 0:wire, :] = back[level, me, part]
        inverse(me, ret[level, me, 0], ret[level, me, 1])

        if level == 0:
            for copy in volume[1:]:
                copy.wait()
            unpack_parcels()

        def arrive_back(peer):
            remote(
                back.at[level, me],
                ret.at[level, peer, :, pl.ds(0, wire), :],
                send_sem.at[level, 1, me],
                recv_sem.at[level, 1, peer],
                {"lat": peer},
            ).wait_recv()
            inverse(peer, ret[level, peer, 0], ret[level, peer, 1])

        each_peer(arrive_back)

        def screened(start):
            values = [
                (wide[d, pl.ds(start, chunk), 0:width], wide[d, pl.ds(start, chunk), width:])
                for d in range(lanes)
            ]
            for a, (real, imag) in enumerate(short_dft(values, 1)):
                cols = slice(a * width, (a + 1) * width)
                gap = slow[level, pl.ds(start, chunk), cols] - base[level][0:1, :]
                sine, cosine = sincos(depth_spacing * omega * gap)
                yield cols, (real * cosine - imag * sine, real * sine + imag * cosine)

        def join_rows(at, carry):
            start = pl.multiple_of(at * chunk, chunk)
            for cols, pair in screened(start):
                for part, value in enumerate(pair):
                    field[0, part, pl.ds(own + start, chunk), cols] = value
            return carry

        lax.fori_loop(0, rows // chunk, join_rows, 0)
        for cols, pair in screened(rows):
            for part, value in enumerate(pair):
                field[0, part, own - stencils : own, cols] = value[0:stencils] * inside_first
                field[0, part, own + rows : own + rows + stencils, cols] = (
                    value[stencils : 2 * stencils] * inside_last
                )

        lane = lax.broadcasted_iota(jnp.int32, (chunk, wide_y), 1)

        def neighbours(ref_at, part, start, center):
            left_one = jnp.where(lane == 0, 0.0, pltpu.roll(center, 1, axis=1))
            right_one = jnp.where(
                lane == wide_y - 1, 0.0, pltpu.roll(center, wide_y - 1, axis=1)
            )
            return (
                field[ref_at, part, start - 1 : start - 1 + chunk, :]
                + field[ref_at, part, start + 1 : start + 1 + chunk, :]
                + left_one
                + right_one
                - 4.0 * center
            )

        for stencil in range(stencils):
            now, later = stencil % 2, (stencil + 1) % 2
            final = stencil == stencils - 1
            for start in range(own if final else top, own + rows if final else top + ext, chunk):
                real = field[now, 0, start : start + chunk, :]
                imag = field[now, 1, start : start + chunk, :]
                weight = coefs[level, stencil, start - top : start - top + chunk, :]
                new_real = real - weight * neighbours(now, 1, start, imag)
                field[later, 0, start : start + chunk, :] = new_real
                if final:
                    image[level, start - own : start - own + chunk, :] = new_real
                field[later, 1, start : start + chunk, :] = imag + weight * neighbours(
                    now, 0, start, real
                )

        @pl.when(core != level)
        def _():
            swap.start()

    def drain(peer):
        for level in range(levels):
            for way, src, dst in (
                (0, sent.at[level, peer], got.at[level, me]),
                (1, back.at[level, peer], ret.at[level, me, :, pl.ds(0, wire), :]),
            ):
                if (level, way) != (0, 0):
                    remote(
                        src,
                        dst,
                        send_sem.at[level, way, peer],
                        recv_sem.at[level, way, me],
                        {"lat": peer},
                    ).wait_send()

    def drain_first(peer):
        remote(
            sent.at[0, peer],
            got.at[0, me],
            send_sem.at[0, 0, peer],
            recv_sem.at[0, 0, me],
            {"lat": peer},
        ).wait_send()

    each_peer(drain)
    each_peer(drain_first, 0, gated)
    each_peer(drain_first, gated + 1)
    swap.wait()
    out[0] = image[core] + image_in[...]


def fused(
    surface, slowness, stencil_coef, base_slowness, base_index, frequency_table, slot_frequency
):
    lanes = lax.axis_size("lat")
    sections = lax.axis_size("depth")
    rows, wide_y = surface.shape[2:]
    stencils = stencil_coef.shape[0]
    width = wide_y // lanes
    halo = -(-stencils // tile_rows) * tile_rows
    ext = rows + 2 * halo
    levels = sections
    parcel = -(-stencils * (stencils + 1) // (2 * tile_rows)) * tile_rows
    f32, bf16 = jnp.float32, jnp.bfloat16
    vmem, smem = pltpu.VMEM, pltpu.SMEM
    sem = pltpu.SemaphoreType.DMA
    anywhere = pl.BlockSpec(memory_space=pl.ANY)
    scalar = pl.BlockSpec(memory_space=smem)
    return pl.pallas_call(
        migrate_kernel,
        out_shape=jax.ShapeDtypeStruct((1, rows, wide_y), f32),
        in_specs=[anywhere] * 3 + [scalar] * 4,
        out_specs=pl.BlockSpec(memory_space=vmem),
        scratch_shapes=[
            vmem((2, 2, ext + 2 * tile_rows, wide_y), f32),
            vmem((lanes, 2 * rows, 2 * width), bf16),
            vmem((lanes, 2 * rows, 2 * width), bf16),
            vmem((lanes, 2 * rows, 2 * width), bf16),
            vmem((lanes, 2 * rows, 2 * width), bf16),
            vmem((lanes, 2 * rows, width), f32),
            vmem((lanes, 2 * rows, width), f32),
            vmem((lanes, 2 * rows, width), f32),
            vmem((levels, lanes, 2 * rows, width), f32),
            vmem((levels, lanes, 2 * rows, width), f32),
            vmem((levels, lanes, 2, rows + tile_rows, width), f32),
            vmem((levels, lanes, 2, rows + chunk, width), f32),
            vmem((lanes, rows + chunk, 2 * width), f32),
            vmem((levels, stencils, ext, wide_y), f32),
            vmem((levels, rows + chunk, wide_y), f32),
            vmem((2, parcel, wide_y), f32),
            vmem((levels, 2, parcel, wide_y), f32),
            vmem((levels, tile_rows, tile_lanes), f32),
            vmem((levels, rows, wide_y), f32),
            vmem((rows, wide_y), f32),
            sem((3,)),
            sem((6,)),
            sem((6,)),
            sem((2,)),
            sem((levels, 2, lanes)),
            sem((levels, 2, lanes)),
            sem((2,)),
        ],
        compiler_params=pltpu.CompilerParams(
            collective_id=0, has_side_effects=True, vmem_limit_bytes=60 * 2**20
        ),
    )(surface, slowness, stencil_coef, base_slowness, base_index, frequency_table, slot_frequency)


def migrate(*arrays):
    surface, slowness, stencil_coef = arrays[:3]
    lanes = lax.axis_size("lat")
    sections = lax.axis_size("depth")
    rows, wide_y = surface.shape[2:]
    fits = (
        rows * lanes == wide_y
        and rows == tile_lanes
        and lanes > 1
        and lanes & (lanes - 1) == 0
        and sections == 2
        and surface.shape[0] == sections
        and slowness.shape[0] == 1
        and 0 < 2 * stencil_coef.shape[0] <= tile_rows
    )
    return fused(*arrays) if fits else shards(*arrays)


def solution(mesh):
    placed = (
        P("shots", None, "lat", None),
        P("depth", "lat", None),
        P(None, "depth", "lat", None),
        P(),
        P("depth"),
        P(),
        P("shots"),
    )
    return jax.shard_map(
        migrate,
        mesh=mesh,
        in_specs=placed,
        out_specs=P(("shots", "depth"), "lat", None),
        check_vma=False,
    )
```

profile of v0, /device:TPU:1, one launch (start us, length us, event | category | flops | bytes accessed | tf_op | source)
XLA Modules:
  0.0 118.0 jit_solution(15838769153281373062)
XLA Ops:
  0.7 115.4 %shard_map.73 = f32[1,128,1024]{2,1,0:T(8,128)} custom-call(f32[2,2,128,1024]{3,2,1,0:T(8,128)} %surface.1, f32[1,128,1024]{2,1,0:T(8,128)} %slowness.1, f32[3,1,128,1024]{3,2,1,0:T(8,128)} %coef.1, f32[8]{0:T(128)} %base_table.1, s32[1]{0:T(128)S(6)} %copy.9.base_index, f32[16]{0:T(128)} %freq_table.1, s32[2]{0:T(128)} %slot_freq.1), custom_call_target="tpu_custom_call" | custom-call | tf_op jit(solution)/shard_map/pallas_call | solution.py:818
  116.1 1.9 %copy.10 = f32[1,128,1024]{2,1,0:T(8,128)} copy(f32[1,128,1024]{2,1,0:T(8,128)} %shard_map.73) | data formatting | bytes 1048576
where the time goes:
time: 118 us
  Pallas kernels  115 us (97%)
  local copies, waits for them, and re-layouts  1.89 us (2%)
    pallas_call x1, Pallas kernels, fused(): pl.pallas_call(migrate_kernel, out_shape=jax.ShapeDtypeStruct((1, rows, w...  115 us

commit v1 on v0

--- a/solution.py
+++ b/solution.py
@@ -181,7 +181,7 @@
 tile_rows = 8
 tile_lanes = 128
 chunk = 16
-gate_step = 3
+gate_step = 1
 
 
 def times_root(value, power, count, sign):
@@ -294,6 +294,8 @@
     send_sem,
     recv_sem,
     image_sem,
+    turn,
+    screen,
 ):
     lanes, rows2, width = short.shape
     rows = rows2 // 2
@@ -519,6 +521,27 @@
         lax.fori_loop(low, high, at, 0)
 
     gated = min(gate_step, lanes - 2)
+
+    def take_turn(phase):
+        @pl.when((core == 1) | (phase > 0))
+        def _():
+            pl.semaphore_wait(turn.at[2 * phase + core], 1)
+
+    def pass_turn(phase, sent_to):
+        def one(peer):
+            sent_to(peer).wait_send()
+
+        each_peer(one, 0, gated + 1)
+
+        @pl.when((core == 0) | (phase < 2 * levels - 1))
+        def _():
+            pl.semaphore_signal(
+                turn.at[2 * phase + core + 1],
+                inc=1,
+                device_id={"depth": other},
+                device_id_type=MESH,
+            )
+
     volume = volume_copies()
     swap = remote(
         image.at[other], image_in, image_sem.at[0], image_sem.at[1], {"depth": other}
@@ -580,6 +603,7 @@
             def _():
                 prepare()
 
+        take_turn(2 * level)
         each_peer(send_forward)
         if level == 0:
             table(me, fwd_hi, fwd_lo, False)
@@ -598,9 +622,9 @@
             def _():
                 prepare()
 
-            there(peer_at(gated)).wait_send()
         else:
             make_phase(level)
+        pass_turn(2 * level, there)
 
         def arrive_forward(peer):
             remote(
@@ -635,8 +659,11 @@
             return made[:, 0:width] + made[:, width:] + mul(lo_table, hi)
 
         def column(e, carry):
-            spec = left(bwd_hi[e], bwd_lo[e], short[e])
-            real, imag = spec[:rows], spec[rows:]
+            after[e] = left(bwd_hi[e], bwd_lo[e], short[e])
+            return carry
+
+        def shifted(e, carry):
+            real, imag = after[e, 0:rows, :], after[e, rows:, :]
             shift_real, shift_imag = phase[e, 0:rows, :], phase[e, rows:, :]
             moved = jnp.concatenate(
                 [
@@ -648,7 +675,8 @@
             after[e] = left(fwd_hi[e], fwd_lo[e], moved)
             return carry
 
-        lax.fori_loop(0, lanes, column, 0)
+        lax.fori_loop(0, lanes, column, 0, unroll=2)
+        lax.fori_loop(0, lanes, shifted, 0, unroll=2)
 
         def join_columns(at, carry):
             start = pl.multiple_of(at * chunk, chunk)
@@ -680,6 +708,7 @@
                 {"lat": peer},
             )
 
+        take_turn(2 * level + 1)
         each_peer(lambda peer: home(peer).start())
 
         def inverse(d, real, imag):
@@ -689,11 +718,24 @@
         for part in range(2):
             ret[level, me, part, 0:wire, :] = back[level, me, part]
         inverse(me, ret[level, me, 0], ret[level, me, 1])
+        pass_turn(2 * level + 1, home)
 
         if level == 0:
             for copy in volume[1:]:
                 copy.wait()
             unpack_parcels()
+
+        def make_screen(at, carry):
+            start = pl.multiple_of(at * chunk, chunk)
+            for a in range(lanes):
+                cols = slice(a * width, (a + 1) * width)
+                gap = slow[level, pl.ds(start, chunk), cols] - base[level][0:1, :]
+                sine, cosine = sincos(depth_spacing * omega * gap)
+                screen[0, pl.ds(start, chunk), cols] = cosine
+                screen[1, pl.ds(start, chunk), cols] = sine
+            return carry
+
+        lax.fori_loop(0, rows // chunk + 1, make_screen, 0)
 
         def arrive_back(peer):
             remote(
@@ -714,8 +756,8 @@
             ]
             for a, (real, imag) in enumerate(short_dft(values, 1)):
                 cols = slice(a * width, (a + 1) * width)
-                gap = slow[level, pl.ds(start, chunk), cols] - base[level][0:1, :]
-                sine, cosine = sincos(depth_spacing * omega * gap)
+                cosine = screen[0, pl.ds(start, chunk), cols]
+                sine = screen[1, pl.ds(start, chunk), cols]
                 yield cols, (real * cosine - imag * sine, real * sine + imag * cosine)
 
         def join_rows(at, carry):
@@ -773,27 +815,15 @@
                 (0, sent.at[level, peer], got.at[level, me]),
                 (1, back.at[level, peer], ret.at[level, me, :, pl.ds(0, wire), :]),
             ):
-                if (level, way) != (0, 0):
-                    remote(
-                        src,
-                        dst,
-                        send_sem.at[level, way, peer],
-                        recv_sem.at[level, way, me],
-                        {"lat": peer},
-                    ).wait_send()
-
-    def drain_first(peer):
-        remote(
-            sent.at[0, peer],
-            got.at[0, me],
-            send_sem.at[0, 0, peer],
-            recv_sem.at[0, 0, me],
-            {"lat": peer},
-        ).wait_send()
-
-    each_peer(drain)
-    each_peer(drain_first, 0, gated)
-    each_peer(drain_first, gated + 1)
+                remote(
+                    src,
+                    dst,
+                    send_sem.at[level, way, peer],
+                    recv_sem.at[level, way, me],
+                    {"lat": peer},
+                ).wait_send()
+
+    each_peer(drain, gated + 1)
     swap.wait()
     out[0] = image[core] + image_in[...]
 
@@ -813,11 +843,11 @@
     f32, bf16 = jnp.float32, jnp.bfloat16
     vmem, smem = pltpu.VMEM, pltpu.SMEM
     sem = pltpu.SemaphoreType.DMA
-    anywhere = pl.BlockSpec(memory_space=pl.ANY)
+    anywhere = pl.BlockSpec(memory_space=pltpu.HBM)
     scalar = pl.BlockSpec(memory_space=smem)
     return pl.pallas_call(
         migrate_kernel,
-        out_shape=jax.ShapeDtypeStruct((1, rows, wide_y), f32),
+        out_shape=vmem((1, rows, wide_y), f32),
         in_specs=[anywhere] * 3 + [scalar] * 4,
         out_specs=pl.BlockSpec(memory_space=vmem),
         scratch_shapes=[
@@ -848,9 +878,11 @@
             sem((levels, 2, lanes)),
             sem((levels, 2, lanes)),
             sem((2,)),
+            pltpu.SemaphoreType.REGULAR((4 * levels,)),
+            vmem((2, rows + chunk, wide_y), f32),
         ],
         compiler_params=pltpu.CompilerParams(
-            collective_id=0, has_side_effects=True, vmem_limit_bytes=60 * 2**20
+            collective_id=0, has_side_effects=True, vmem_limit_bytes=62 * 2**20
         ),
     )(surface, slowness, stencil_coef, base_slowness, base_index, frequency_table, slot_frequency)
 

time: 118 us -> 112 us (0.949)
  Pallas kernels: 115 us -> 110 us
    pallas_call x1, Pallas kernels: 115 us -> 110 us  [fused(): pl.pallas_call(migrate_kernel, out_shape=vmem((1, rows, wide_y), f32), in...]
where the time goes in v1:
time: 112 us; the launch traced here: 111 us
  Pallas kernels  110 us (98%)
    pallas_call x1, Pallas kernels, fused(): pl.pallas_call(migrate_kernel, out_shape=vmem((1, rows, wide_y), f32), in...  110 us

profile of v1, /device:TPU:1, one launch (start us, length us, event | category | flops | bytes accessed | tf_op | source)
XLA Modules:
  0.0 111.2 jit_solution(4633159861976765383)
XLA Ops:
  0.7 109.7 %shard_map.73 = f32[1,128,1024]{2,1,0:T(8,128)S(1)} custom-call(f32[2,2,128,1024]{3,2,1,0:T(8,128)} %surface.1, f32[1,128,1024]{2,1,0:T(8,128)} %slowness.1, f32[3,1,128,1024]{3,2,1,0:T(8,128)} %coef.1, f32[8]{0:T(128)} %base_table.1, s32[1]{0:T(128)S(6)} %copy.10.base_index, f32[16]{0:T(128)} %freq_table.1, s32[2]{0:T(128)} %slot_freq.1), custom_call_target="tpu_custom_call" | custom-call | tf_op jit(solution)/shard_map/pallas_call | solution.py:848
  110.4 0.8 copy.9

commit v2 on v1

--- a/solution.py
+++ b/solution.py
@@ -181,7 +181,7 @@
 tile_rows = 8
 tile_lanes = 128
 chunk = 16
-gate_step = 1
+gate_step = 2
 
 
 def times_root(value, power, count, sign):
@@ -393,8 +393,6 @@
 
         lax.fori_loop(0, lanes, body, 0)
 
-    load.wait()
-
     def remote(src, dst, send, recv, device):
         return pltpu.make_async_remote_copy(
             src_ref=src,
@@ -523,6 +521,9 @@
     gated = min(gate_step, lanes - 2)
 
     def take_turn(phase):
+        if phase == 2 * levels - 1:
+            return
+
         @pl.when((core == 1) | (phase > 0))
         def _():
             pl.semaphore_wait(turn.at[2 * phase + core], 1)
@@ -533,7 +534,10 @@
 
         each_peer(one, 0, gated + 1)
 
-        @pl.when((core == 0) | (phase < 2 * levels - 1))
+        if phase == 2 * levels - 1:
+            return
+
+        @pl.when((core == 0) | (phase < 2 * levels - 2))
         def _():
             pl.semaphore_signal(
                 turn.at[2 * phase + core + 1],
@@ -548,6 +552,14 @@
     )
     for level in range(levels):
         source = 0 if level == 0 else stencils % 2
+
+        if level == 0:
+
+            @pl.when(core == 0)
+            def _():
+                table(peer_at(0), fwd_hi, fwd_lo, False)
+
+            load.wait()
 
         def split_rows(at, carry):
             start = pl.multiple_of(at * chunk, chunk)
@@ -583,8 +595,6 @@
             )
 
         def send_forward(peer):
-            if level == 0:
-                table(peer, fwd_hi, fwd_lo, False)
             made = forward(peer)
             sent[level, peer, 0:rows, :] = made[:, 0:width]
             sent[level, peer, rows:, :] = made[:, width:]
@@ -603,10 +613,32 @@
             def _():
                 prepare()
 
+        if level == 0:
+
+            @pl.when(core == 1)
+            def _():
+                tables(fwd_hi, fwd_lo, False)
+
         take_turn(2 * level)
-        each_peer(send_forward)
         if level == 0:
-            table(me, fwd_hi, fwd_lo, False)
+
+            @pl.when(core == 0)
+            def _():
+                send_forward(peer_at(0))
+
+                def with_table(peer):
+                    table(peer, fwd_hi, fwd_lo, False)
+                    send_forward(peer)
+
+                each_peer(with_table, 1)
+                table(me, fwd_hi, fwd_lo, False)
+
+            @pl.when(core == 1)
+            def _():
+                each_peer(send_forward)
+
+        else:
+            each_peer(send_forward)
         made = forward(me)
         got[level, me, 0:rows, :] = made[:, 0:width]
         got[level, me, rows:, :] = made[:, width:]
@@ -622,8 +654,6 @@
             def _():
                 prepare()
 
-        else:
-            make_phase(level)
         pass_turn(2 * level, there)
 
         def arrive_forward(peer):
@@ -736,6 +766,8 @@
             return carry
 
         lax.fori_loop(0, rows // chunk + 1, make_screen, 0)
+        if level + 1 < levels:
+            make_phase(level + 1)
 
         def arrive_back(peer):
             remote(
@@ -749,26 +781,26 @@
 
         each_peer(arrive_back)
 
-        def screened(start):
+        def screened(start, size):
             values = [
-                (wide[d, pl.ds(start, chunk), 0:width], wide[d, pl.ds(start, chunk), width:])
+                (wide[d, pl.ds(start, size), 0:width], wide[d, pl.ds(start, size), width:])
                 for d in range(lanes)
             ]
             for a, (real, imag) in enumerate(short_dft(values, 1)):
                 cols = slice(a * width, (a + 1) * width)
-                cosine = screen[0, pl.ds(start, chunk), cols]
-                sine = screen[1, pl.ds(start, chunk), cols]
+                cosine = screen[0, pl.ds(start, size), cols]
+                sine = screen[1, pl.ds(start, size), cols]
                 yield cols, (real * cosine - imag * sine, real * sine + imag * cosine)
 
         def join_rows(at, carry):
             start = pl.multiple_of(at * chunk, chunk)
-            for cols, pair in screened(start):
+            for cols, pair in screened(start, chunk):
                 for part, value in enumerate(pair):
                     field[0, part, pl.ds(own + start, chunk), cols] = value
             return carry
 
         lax.fori_loop(0, rows // chunk, join_rows, 0)
-        for cols, pair in screened(rows):
+        for cols, pair in screened(rows, tile_rows):
             for part, value in enumerate(pair):
                 field[0, part, own - stencils : own, cols] = value[0:stencils] * inside_first
                 field[0, part, own + rows : own + rows + stencils, cols] = (

time: 112 us -> 110 us (0.982)
  Pallas kernels: 110 us -> 108 us
    pallas_call x1, Pallas kernels: 110 us -> 108 us  [fused(): pl.pallas_call(migrate_kernel, out_shape=vmem((1, rows, wide_y), f32), in...]
where the time goes in v2:
time: 110 us; the launch traced here: 109 us
  Pallas kernels  108 us (98%)
    pallas_call x1, Pallas kernels, fused(): pl.pallas_call(migrate_kernel, out_shape=vmem((1, rows, wide_y), f32), in...  108 us

profile of v2, /device:TPU:1, one launch (start us, length us, event | category | flops | bytes accessed | tf_op | source)
XLA Modules:
  0.0 109.4 jit_solution(17651057946089925399)
XLA Ops:
  0.7 107.9 %shard_map.73 = f32[1,128,1024]{2,1,0:T(8,128)S(1)} custom-call(f32[2,2,128,1024]{3,2,1,0:T(8,128)} %surface.1, f32[1,128,1024]{2,1,0:T(8,128)} %slowness.1, f32[3,1,128,1024]{3,2,1,0:T(8,128)} %coef.1, f32[8]{0:T(128)} %base_table.1, s32[1]{0:T(128)S(6)} %copy.10.base_index, f32[16]{0:T(128)} %freq_table.1, s32[2]{0:T(128)} %slot_freq.1), custom_call_target="tpu_custom_call" | custom-call | tf_op jit(solution)/shard_map/pallas_call | solution.py:880
  108.6 0.8 copy.9

commit v3 on v2

--- a/solution.py
+++ b/solution.py
@@ -830,12 +830,14 @@
                 imag = field[now, 1, start : start + chunk, :]
                 weight = coefs[level, stencil, start - top : start - top + chunk, :]
                 new_real = real - weight * neighbours(now, 1, start, imag)
-                field[later, 0, start : start + chunk, :] = new_real
+                if not final or level < levels - 1:
+                    field[later, 0, start : start + chunk, :] = new_real
                 if final:
                     image[level, start - own : start - own + chunk, :] = new_real
-                field[later, 1, start : start + chunk, :] = imag + weight * neighbours(
-                    now, 0, start, real
-                )
+                if not final or level < levels - 1:
+                    field[later, 1, start : start + chunk, :] = imag + weight * neighbours(
+                        now, 0, start, real
+                    )
 
         @pl.when(core != level)
         def _():

time: 110 us -> 109 us (level)
  no operation moved by 1% of the time
where the time goes in v3:
time: 109 us
  Pallas kernels  108 us (99%)
    pallas_call x1, Pallas kernels, fused(): pl.pallas_call(migrate_kernel, out_shape=vmem((1, rows, wide_y), f32), in...  108 us

profile of v3, /device:TPU:1, one launch (start us, length us, event | category | flops | bytes accessed | tf_op | source)
XLA Modules:
  0.0 109.0 jit_solution(4410347761691371605)
XLA Ops:
  0.7 107.5 %shard_map.73 = f32[1,128,1024]{2,1,0:T(8,128)S(1)} custom-call(f32[2,2,128,1024]{3,2,1,0:T(8,128)} %surface.1, f32[1,128,1024]{2,1,0:T(8,128)} %slowness.1, f32[3,1,128,1024]{3,2,1,0:T(8,128)} %coef.1, f32[8]{0:T(128)} %base_table.1, s32[1]{0:T(128)S(6)} %copy.10.base_index, f32[16]{0:T(128)} %freq_table.1, s32[2]{0:T(128)} %slot_freq.1), custom_call_target="tpu_custom_call" | custom-call | tf_op jit(solution)/shard_map/pallas_call | solution.py:882
  108.2 0.8 copy.9
